TPU v7x, 32 devices: a whole 2x2x4 slice. The times are simulated.
32 devices in a mesh: dp: 4 (over y, core), row: 2 (over x), col: 4 (over z).
Axes of the slice: x: 2, y: 2, z: 4, core: 2. Of those that a mesh axis runs over, the one named last changes fastest.
Arguments:
- tokens: bfloat16 [16384, 1152], P(('dp', 'col')), may hold values from -6 to 6
- segment_ids: int32 [16384], P(('dp', 'col')), may hold values from -1 to 10, as said below
- doc_starts: int32 [4, 12], P('dp'), may hold values from 0 to 4096, as said below
- norm1_gain: bfloat16 [1152], P('col'), may hold values from 0.25 to 1.75
- norm2_gain: bfloat16 [1152], P('col'), may hold values from 0.25 to 1.75
- query_key_value_weight: bfloat16 [1152, 6, 320], P('col', 'row'), may hold values from -0.1875 to 0.1875
- output_weight: bfloat16 [1152, 6, 192], P('col', 'row'), may hold values from -2 to 2
- w_gate_up: bfloat16 [1152, 2, 3072], P('col', None, 'row'), may hold values from -0.1875 to 0.1875
- w_down: bfloat16 [1152, 3072], P('col', 'row'), may hold values from -0.21875 to 0.21875
- cotangent: bfloat16 [16384, 1152], P(('dp', 'col')), may hold values from -6 to 6
Outputs:
- layer_output: bfloat16 [16384, 1152], P(('dp', 'col'))
- input_grad: float32 [16384, 1152], P(('dp', 'col'))
- norm1_gain_grad: float32 [1152], P('col')
- norm2_gain_grad: float32 [1152], P('col')
- w_qkv_grad: float32 [1152, 6, 320], P('col', 'row')
- w_out_grad: float32 [1152, 6, 192], P('col', 'row')
- w_gate_up_grad: float32 [1152, 2, 3072], P('col', None, 'row')
- w_down_grad: float32 [1152, 3072], P('col', 'row')
Inputs may be any that keep to these rules, and one draw needn't show every extreme that they name: `segment_ids`: each sequence of 4096 tokens is a run of whole documents numbered 0, 1, 2, ... in order, each of 200 to 2000 tokens, the first exactly 2000, followed by at least one padding token with segment -1. doc_starts[s, d] is the index within sequence s of the first token of its document d; slots after its last document hold 4096.
All inputs are finite; a program needn't handle non-finite values.
Results may differ from a plain program's by a relative error of at most 0.014.
Values may be sent and summed in bfloat16 or wider, within the bound.
No kernel may reach another device: no remote copies, remote signals or barrier semaphores. Data moves between devices by JAX's collectives and lax.ppermute only.
A program may use at most 192 MiB of HBM per device.

v0:
```python
import math
import jax
import jax.numpy as jnp
from jax import lax
from jax.sharding import PartitionSpec as P

QUERY_HEADS = 18
KEY_VALUE_HEADS = 6
HEAD_WIDTH = 64
SEQ_CAP = 4096
DOC_CAP = 2000
epsilon = 1e-05
rope_base = 10000.0
masked_score = -1e30


def shifted(value, axis, steps):
    count = lax.axis_size(axis)
    leading, last = (max(0, -steps), min(count, count - steps))
    return lax.ppermute(value, axis, [(source, source + steps) for source in range(leading, last)])


def rms_parts(values):
    inverse = lax.rsqrt(jnp.mean(values * values, axis=-1, keepdims=True) + epsilon)
    return (values * inverse, inverse)


def rms_back(grad_normed, normed, inverse):
    return inverse * (grad_normed - normed * jnp.mean(grad_normed * normed, axis=-1, keepdims=True))


def rope_tables(position):
    half_width = HEAD_WIDTH // 2
    frequency = jnp.power(rope_base, -2.0 * jnp.arange(half_width, dtype=jnp.float32) / HEAD_WIDTH)
    angles = position[:, None] * frequency[None, :]
    return (jnp.cos(angles), jnp.sin(angles))


def rotate_pairs(values, cosine_values, sine_values):
    half_width = values.shape[-1] // 2
    lower_half = values[..., :half_width]
    upper_half = values[..., half_width:]
    return jnp.concatenate(
        [
            lower_half * cosine_values - upper_half * sine_values,
            upper_half * cosine_values + lower_half * sine_values,
        ],
        axis=-1,
    )


def local(
    tokens,
    segment_ids,
    doc_starts,
    norm1_gain,
    norm2_gain,
    query_key_value_weight,
    output_weight,
    w_gate_up,
    w_down,
    cotangent,
):
    tok_count = tokens.shape[0]
    column = lax.axis_index("col")
    seq_len = min(SEQ_CAP, tok_count * lax.axis_size("col"))
    doc_most = min(DOC_CAP, seq_len // 2)
    back_shards = (doc_most + tok_count - 2) // tok_count
    rows_per_block = min(512, tok_count)
    block_list = tok_count // rows_per_block
    heads_local = query_key_value_weight.shape[1]
    group_width = QUERY_HEADS // KEY_VALUE_HEADS
    query_feature_width = group_width * HEAD_WIDTH
    score_scale = 1.0 / math.sqrt(HEAD_WIDTH)
    gain_one, gain_two, full_qkv, full_out, full_gate_up, full_down = (
        lax.all_gather(norm1_gain, "col", axis=0, tiled=True),
        lax.all_gather(norm2_gain, "col", axis=0, tiled=True),
        lax.all_gather(query_key_value_weight, "col", axis=0, tiled=True),
        lax.all_gather(output_weight, "col", axis=0, tiled=True),
        lax.all_gather(w_gate_up, "col", axis=0, tiled=True),
        lax.all_gather(w_down, "col", axis=0, tiled=True),
    )
    gain_one = gain_one.astype(jnp.float32)
    gain_two = gain_two.astype(jnp.float32)
    offset = column * tok_count
    global_rows = offset + jnp.arange(tok_count, dtype=jnp.int32)
    seq_index = offset // seq_len
    in_seq = global_rows - seq_index * seq_len
    chosen = jnp.arange(doc_starts.shape[0], dtype=jnp.int32) == seq_index
    start_row = jnp.sum(jnp.where(chosen[:, None], doc_starts, 0), axis=0)
    matches = segment_ids[:, None] == jnp.arange(doc_starts.shape[1], dtype=jnp.int32)[None, :]
    begins = jnp.sum(jnp.where(matches, start_row[None, :], 0), axis=1)
    begin_global = seq_index * seq_len + begins
    cosine_values, sine_values = rope_tables((in_seq - begins).astype(jnp.float32))
    layer_input = tokens.astype(jnp.float32)
    normed_one, inverse_one = rms_parts(layer_input)
    input_one = (normed_one * gain_one).astype(jnp.bfloat16)
    projected_rows = jnp.einsum(
        "td,dhe->the", input_one, full_qkv, preferred_element_type=jnp.float32
    )
    query_raw = projected_rows[..., :query_feature_width].reshape(
        tok_count, heads_local, group_width, HEAD_WIDTH
    )
    query_matrix = rotate_pairs(
        query_raw, cosine_values[:, None, None, :], sine_values[:, None, None, :]
    ).astype(jnp.bfloat16)
    key_rows = rotate_pairs(
        projected_rows[..., query_feature_width : query_feature_width + HEAD_WIDTH],
        cosine_values[:, None, :],
        sine_values[:, None, :],
    ).astype(jnp.bfloat16)
    value_rows = projected_rows[..., query_feature_width + HEAD_WIDTH :].astype(jnp.bfloat16)
    segment_float = segment_ids.astype(jnp.bfloat16)
    key_parts = [key_rows]
    value_parts = [value_rows]
    segment_parts = [segment_float]
    for distance in range(1, back_shards + 1):
        moved = shifted((key_rows, value_rows, segment_float), "col", distance)
        key_parts.insert(0, moved[0])
        value_parts.insert(0, moved[1])
        segment_parts.insert(0, moved[2])
    key_all = jnp.concatenate(key_parts, axis=0)
    value_all = jnp.concatenate(value_parts, axis=0)
    segment_all = jnp.concatenate(segment_parts, axis=0)
    key_global = offset - back_shards * tok_count + jnp.arange(key_all.shape[0], dtype=jnp.int32)
    same_seq = jnp.floor_divide(key_global, seq_len) == seq_index
    key_padding = (segment_all < 0) & same_seq
    row_blocks = global_rows.reshape(block_list, rows_per_block)
    segment_blocks = segment_float.reshape(block_list, rows_per_block)
    begin_blocks = begin_global.reshape(block_list, rows_per_block)
    query_heads = jnp.moveaxis(
        query_matrix.reshape(block_list, rows_per_block, heads_local, group_width, HEAD_WIDTH), 2, 0
    )
    key_heads = jnp.moveaxis(key_all, 1, 0)
    value_heads = jnp.moveaxis(value_all, 1, 0)

    def scores_for(query_block, head_keys, rows_block, segment_block, begin_block):
        live_query = segment_block[:, None] >= 0
        causal = key_global[None, :] <= rows_block[:, None]
        in_doc = same_seq[None, :] & (key_global[None, :] >= begin_block[:, None])
        allowed = causal & jnp.where(live_query, in_doc, key_padding[None, :])
        allowed = allowed | (key_global[None, :] == rows_block[:, None])
        scores = (
            jnp.einsum("qgd,kd->gqk", query_block, head_keys, preferred_element_type=jnp.float32)
            * score_scale
        )
        return (scores, allowed)

    def forward_head(packed):
        head_queries, head_keys, head_values = packed

        def forward_block(inner):
            query_block, rows_block, segment_block, begin_block = inner
            scores, allowed = scores_for(
                query_block, head_keys, rows_block, segment_block, begin_block
            )
            scores = jnp.where(allowed[None], scores, masked_score)
            row_peak = jnp.max(scores, axis=-1, keepdims=True)
            exponents = jnp.exp(scores - row_peak)
            denominator = jnp.sum(exponents, axis=-1, keepdims=True)
            probs_low = (exponents / denominator).astype(jnp.bfloat16)
            attended_context = jnp.einsum(
                "gqk,kd->qgd", probs_low, head_values, preferred_element_type=jnp.float32
            )
            return (attended_context, (row_peak + jnp.log(denominator))[..., 0])

        return lax.map(forward_block, (head_queries, row_blocks, segment_blocks, begin_blocks))

    contexts, log_totals = lax.map(forward_head, (query_heads, key_heads, value_heads))
    context_low = (
        jnp.moveaxis(contexts, 0, 2)
        .reshape(tok_count, heads_local, query_feature_width)
        .astype(jnp.bfloat16)
    )
    attention = lax.psum(
        jnp.einsum("the,dhe->td", context_low, full_out, preferred_element_type=jnp.float32), "row"
    )
    residual = layer_input + attention
    normed_two, inverse_two = rms_parts(residual)
    input_two = (normed_two * gain_two).astype(jnp.bfloat16)
    gate_up = jnp.einsum("td,dcf->tcf", input_two, full_gate_up, preferred_element_type=jnp.float32)
    gate_value = gate_up[:, 0]
    up_value = gate_up[:, 1]
    gate_act = jax.nn.silu(gate_value)
    hidden = (gate_act * up_value).astype(jnp.bfloat16)
    feed = lax.psum(
        jnp.einsum("tf,df->td", hidden, full_down, preferred_element_type=jnp.float32).astype(
            jnp.bfloat16
        ),
        "row",
    ).astype(jnp.float32)
    layer_output = (residual + feed).astype(jnp.bfloat16)
    back_qkv, back_out, back_gate_up, back_down = (
        lax.all_gather(query_key_value_weight, "col", axis=0, tiled=True),
        lax.all_gather(output_weight, "col", axis=0, tiled=True),
        lax.all_gather(w_gate_up, "col", axis=0, tiled=True),
        lax.all_gather(w_down, "col", axis=0, tiled=True),
    )
    live_rows = (segment_ids >= 0).astype(jnp.float32)
    grad_out = cotangent.astype(jnp.float32) * live_rows[:, None]
    grad_feed = grad_out.astype(jnp.bfloat16)
    down_grad = jnp.einsum("tf,td->df", hidden, grad_feed, preferred_element_type=jnp.float32)
    grad_hidden = jnp.einsum("td,df->tf", grad_feed, back_down, preferred_element_type=jnp.float32)
    sigmoid_gate = jax.nn.sigmoid(gate_value)
    grad_gate = grad_hidden * up_value * sigmoid_gate * (1.0 + gate_value * (1.0 - sigmoid_gate))
    grad_up = grad_hidden * gate_act
    grad_gate_up = jnp.stack([grad_gate, grad_up], axis=1).astype(jnp.bfloat16)
    gate_up_grad = jnp.einsum(
        "td,tcf->dcf", input_two, grad_gate_up, preferred_element_type=jnp.float32
    )
    grad_input_two = lax.psum(
        jnp.einsum("tcf,dcf->td", grad_gate_up, back_gate_up, preferred_element_type=jnp.float32),
        "row",
    )
    gain_two_grad = jnp.sum(grad_input_two * normed_two, axis=0)
    grad_residual = grad_out + rms_back(grad_input_two * gain_two, normed_two, inverse_two)
    grad_attention = grad_residual.astype(jnp.bfloat16)
    out_grad = jnp.einsum(
        "the,td->dhe", context_low, grad_attention, preferred_element_type=jnp.float32
    )
    grad_context = jnp.einsum(
        "td,dhe->the", grad_attention, back_out, preferred_element_type=jnp.float32
    ).astype(jnp.bfloat16)
    grad_heads = jnp.moveaxis(
        grad_context.reshape(block_list, rows_per_block, heads_local, group_width, HEAD_WIDTH), 2, 0
    )

    def backward_head(packed):
        head_queries, head_keys, head_values, head_grads, head_logs = packed

        def backward_block(carry, inner):
            key_acc, value_acc = carry
            query_block, grad_block, log_block, rows_block, segment_block, begin_block = inner
            scores, allowed = scores_for(
                query_block, head_keys, rows_block, segment_block, begin_block
            )
            probs = jnp.where(allowed[None], jnp.exp(scores - log_block[..., None]), 0.0)
            value_acc = value_acc + jnp.einsum(
                "gqk,qgd->kd",
                probs.astype(jnp.bfloat16),
                grad_block,
                preferred_element_type=jnp.float32,
            )
            grad_probs = jnp.einsum(
                "qgd,kd->gqk", grad_block, head_values, preferred_element_type=jnp.float32
            )
            inner_sum = jnp.sum(probs * grad_probs, axis=-1, keepdims=True)
            grad_scores = (probs * (grad_probs - inner_sum)).astype(jnp.bfloat16)
            grad_query = (
                jnp.einsum(
                    "gqk,kd->qgd", grad_scores, head_keys, preferred_element_type=jnp.float32
                )
                * score_scale
            )
            key_acc = (
                key_acc
                + jnp.einsum(
                    "gqk,qgd->kd", grad_scores, query_block, preferred_element_type=jnp.float32
                )
                * score_scale
            )
            return ((key_acc, value_acc), grad_query)

        zero_rows = jnp.zeros(head_keys.shape, jnp.float32)
        (key_acc, value_acc), grad_queries = lax.scan(
            backward_block,
            (zero_rows, zero_rows),
            (head_queries, head_grads, head_logs, row_blocks, segment_blocks, begin_blocks),
        )
        return (grad_queries, key_acc, value_acc)

    grad_queries, key_grads, value_grads = lax.map(
        backward_head, (query_heads, key_heads, value_heads, grad_heads, log_totals)
    )
    key_grads = jnp.moveaxis(key_grads, 0, 1)
    value_grads = jnp.moveaxis(value_grads, 0, 1)
    own_start = back_shards * tok_count
    key_own = key_grads[own_start:]
    value_own = value_grads[own_start:]
    for distance in range(1, back_shards + 1):
        first_row = (back_shards - distance) * tok_count
        returned = (
            shifted(
                key_grads[first_row : first_row + tok_count].astype(jnp.bfloat16), "col", -distance
            ).astype(jnp.float32),
            shifted(
                value_grads[first_row : first_row + tok_count].astype(jnp.bfloat16),
                "col",
                -distance,
            ).astype(jnp.float32),
        )
        key_own = key_own + returned[0]
        value_own = value_own + returned[1]
    grad_query_rows = jnp.moveaxis(grad_queries, 0, 2).reshape(
        tok_count, heads_local, group_width, HEAD_WIDTH
    )
    query_back = rotate_pairs(
        grad_query_rows, cosine_values[:, None, None, :], -sine_values[:, None, None, :]
    ).reshape(tok_count, heads_local, query_feature_width)
    key_back = rotate_pairs(key_own, cosine_values[:, None, :], -sine_values[:, None, :])
    grad_projected = jnp.concatenate([query_back, key_back, value_own], axis=-1).astype(
        jnp.bfloat16
    )
    qkv_grad = jnp.einsum(
        "td,the->dhe", input_one, grad_projected, preferred_element_type=jnp.float32
    )
    grad_input_one = lax.psum(
        jnp.einsum("the,dhe->td", grad_projected, back_qkv, preferred_element_type=jnp.float32),
        "row",
    )
    gain_one_grad = jnp.sum(grad_input_one * normed_one, axis=0)
    input_grad = grad_residual + rms_back(grad_input_one * gain_one, normed_one, inverse_one)
    share_one, share_two, share_qkv, share_out, share_gate_up, share_down = (
        lax.psum_scatter(gain_one_grad, "col", scatter_dimension=0, tiled=True),
        lax.psum_scatter(gain_two_grad, "col", scatter_dimension=0, tiled=True),
        lax.psum_scatter(qkv_grad, "col", scatter_dimension=0, tiled=True),
        lax.psum_scatter(out_grad, "col", scatter_dimension=0, tiled=True),
        lax.psum_scatter(gate_up_grad, "col", scatter_dimension=0, tiled=True),
        lax.psum_scatter(down_grad, "col", scatter_dimension=0, tiled=True),
    )
    total_one, total_two, total_qkv, total_out, total_gate_up, total_down = lax.psum(
        (share_one, share_two, share_qkv, share_out, share_gate_up, share_down), "dp"
    )
    return (
        layer_output,
        input_grad,
        total_one,
        total_two,
        total_qkv,
        total_out,
        total_gate_up,
        total_down,
    )


def solution(mesh):
    placed = (
        P(("dp", "col"), None),
        P(("dp", "col")),
        P("dp", None),
        P("col"),
        P("col"),
        P("col", "row", None),
        P("col", "row", None),
        P("col", None, "row"),
        P("col", "row"),
        P(("dp", "col"), None),
    )
    return jax.shard_map(
        local,
        mesh=mesh,
        in_specs=placed,
        out_specs=(
            P(("dp", "col"), None),
            P(("dp", "col"), None),
            P("col"),
            P("col"),
            P("col", "row", None),
            P("col", "row", None),
            P("col", None, "row"),
            P("col", "row"),
        ),
        check_vma=False,
    )
```

profile of v0, /device:TPU:0, one launch (start us, length us, event | category | flops | bytes accessed | tf_op | source)
XLA Modules:
  0.0 2066.5 jit_solution(14559142088123442937)
XLA Ops:
  35.0 33.1 %all-gather.5.cloned.1.call-done = bf16[1152,3,320]{2,0,1:T(8,128)(2,1)} async-done(((bf16[288,3,320]{2,0,1:T(8,128)(2,1)}), bf16[1152,3,320]{2,0,1:T(8,128)(2,1)}) %all-gather.5.cloned.1.call-update) | async-done | bytes 2211856 | tf_op jit(solution)/shard_map/all_gather | solution.py:78
  95.2 16.9 collective-permute-done.1
  114.1 14.7 collective-permute-done.2
  141.1 120.9 %while.68 = (s32[]{:T(128)}, bf16[3,2,512,3,64]{2,4,3,1,0:T(8,128)(2,1)}, f32[3,2,3,512]{3,2,1,0:T(4,128)}, bf16[3,2,512,3,64]{2,4,3,1,0:T(8,128)(2,1)}, bf16[3,...) while((s32[]{:T(128)}, ...), condition=%wide.region_7.8_spmd.clone.clone.clone, body=%wide.region_2.0_spmd.clone.clone.sunk.clone | while | flops 1275651072 | bytes 67578264 | solution.py:169
  143.9 36.5 %while.67 = (s32[]{:T(128)}, bf16[2,512,3,64]{1,3,2,0:T(8,128)(2,1)S(1)}, f32[2,3,512]{2,1,0:T(4,128)S(1)}, s32[3072]{0:T(1024)S(1)}, s32[2,512]{1,0:T(2,128)S(1...) while((s32[]{:T(128)}, ...), condition=%wide.region_6.6_spmd, body=%wide.region_3.5_spmd.sunk | while | flops 1275592704 | bytes 64383120 | solution.py:167
  184.0 36.5 %while.67 = (s32[]{:T(128)}, bf16[2,512,3,64]{1,3,2,0:T(8,128)(2,1)S(1)}, f32[2,3,512]{2,1,0:T(4,128)S(1)}, s32[3072]{0:T(1024)S(1)}, s32[2,512]{1,0:T(2,128)S(1...) while((s32[]{:T(128)}, ...), condition=%wide.region_6.6_spmd, body=%wide.region_3.5_spmd.sunk | while | flops 1275592704 | bytes 64383120 | solution.py:167
  224.2 36.5 %while.67 = (s32[]{:T(128)}, bf16[2,512,3,64]{1,3,2,0:T(8,128)(2,1)S(1)}, f32[2,3,512]{2,1,0:T(4,128)S(1)}, s32[3072]{0:T(1024)S(1)}, s32[2,512]{1,0:T(2,128)S(1...) while((s32[]{:T(128)}, ...), condition=%wide.region_6.6_spmd, body=%wide.region_3.5_spmd.sunk | while | flops 1275592704 | bytes 64383120 | solution.py:167
  276.0 132.3 %all-reduce.14.cloned.1.call-done = f32[1024,1152]{1,0:T(8,128)} async-done(((f32[1024,1152]{1,0:T(8,128)}), f32[1024,1152]{1,0:T(8,128)}) %all-reduce.14.cloned.1.call-update) | async-done | bytes 4718608 | tf_op jit(solution)/shard_map/psum | solution.py:175
  413.4 125.1 %all-gather.9.cloned.1.call-done = bf16[1152,2,1536]{2,0,1:T(8,128)(2,1)} async-done(((bf16[288,2,1536]{2,0,1:T(8,128)(2,1)}), bf16[1152,2,1536]{2,0,1:T(8,128)(2,1)}) %all-gather.9.cloned.1.call-update) | async-done | bytes 7077904 | tf_op jit(solution)/shard_map/all_gather | solution.py:80
  538.5 15.3 fusion.106
  553.8 54.3 %all-gather.11.cloned.1.call-done = bf16[1152,1536]{1,0:T(8,128)(2,1)} async-done(((bf16[288,1536]{1,0:T(8,128)(2,1)}), bf16[1152,1536]{1,0:T(8,128)(2,1)}) %all-gather.11.cloned.1.call-update) | async-done | bytes 3538960 | tf_op jit(solution)/shard_map/all_gather | solution.py:81
  645.2 105.3 %all-reduce.18.cloned.1.call-done = f32[1024,1152]{1,0:T(8,128)} async-done(((f32[1024,1152]{1,0:T(8,128)}), f32[1024,1152]{1,0:T(8,128)}) %all-reduce.18.cloned.1.call-update) | async-done | bytes 4718608 | tf_op jit(solution)/shard_map/psum | solution.py:211
  756.6 65.5 %all-reduce.16.cloned.1.call-done = bf16[1024,1152]{1,0:T(8,128)(2,1)} async-done(((bf16[1024,1152]{1,0:T(8,128)(2,1)}), bf16[1024,1152]{1,0:T(8,128)(2,1)}) %all-reduce.16.cloned.1.call-update) | async-done | bytes 2359312 | tf_op jit(solution)/shard_map/psum | solution.py:186
  841.4 418.1 %while.70 = (s32[]{:T(128)}, f32[3,2,512,3,64]{2,4,3,1,0:T(8,128)}, f32[3,3072,64]{1,2,0:T(8,128)}, f32[3,3072,64]{1,2,0:T(8,128)}, bf16[3,2,512,3,64]{2,4,3,1,0...) while((s32[]{:T(128)}, f32[3,2,512,3,64]{2,4,3,1,0:T(8,128)}, ...), condition=%wide.region_17.18_spmd.clone.clone.clone, body=%wide.region_13.17_spmd.clone.clone.sunk.clone | while | flops 3102827520 | bytes 211725008 | solution.py:272
  849.8 128.0 %while.69 = (s32[]{:T(128)}, f32[3072,64]{0,1:T(8,128)S(1)}, f32[3072,64]{0,1:T(8,128)}, f32[2,512,3,64]{1,3,2,0:T(8,128)}, s32[3072]{0:T(1024)}, /*index=5*/s32...) while((s32[]{:T(128)}, f32[3072,64]{0,1:T(8,128)S(1)}, ...), condition=%wide.region_16.16_spmd.clone, body=%wide.region_14.15_spmd.clone.sunk | while | flops 3102769152 | bytes 200669552 | solution.py:265
  875.9 18.0 fusion.169
  939.9 17.9 fusion.169
  989.3 127.6 %while.69 = (s32[]{:T(128)}, f32[3072,64]{0,1:T(8,128)S(1)}, f32[3072,64]{0,1:T(8,128)}, f32[2,512,3,64]{1,3,2,0:T(8,128)}, s32[3072]{0:T(1024)}, /*index=5*/s32...) while((s32[]{:T(128)}, f32[3072,64]{0,1:T(8,128)S(1)}, ...), condition=%wide.region_16.16_spmd.clone, body=%wide.region_14.15_spmd.clone.sunk | while | flops 3102769152 | bytes 200669552 | solution.py:265
  1015.2 17.9 fusion.169
  1078.9 17.9 fusion.169
  1128.3 127.6 %while.69 = (s32[]{:T(128)}, f32[3072,64]{0,1:T(8,128)S(1)}, f32[3072,64]{0,1:T(8,128)}, f32[2,512,3,64]{1,3,2,0:T(8,128)}, s32[3072]{0:T(1024)}, /*index=5*/s32...) while((s32[]{:T(128)}, f32[3072,64]{0,1:T(8,128)S(1)}, ...), condition=%wide.region_16.16_spmd.clone, body=%wide.region_14.15_spmd.clone.sunk | while | flops 3102769152 | bytes 200669552 | solution.py:265
  1154.2 17.9 fusion.169
  1217.9 17.9 fusion.169
  1277.7 25.3 %collective-permute-done.7 = bf16[1024,3,64]{0,2,1:T(8,128)(2,1)S(1)} collective-permute-done((bf16[1024,3,64]{0,2,1:T(8,128)(2,1)S(1)}, bf16[1024,3,64]{0,2,1:T(8,128)(2,1)S(1)}, u32[]{:S(2)}, u32[]{:S(2)}) %collective-permute-start.7) | collective-permute-done | bytes 393248 | tf_op jit(solution)/shard_map/ppermute | solution.py:20
  1303.3 15.3 collective-permute-done.9
  1336.3 14.5 fusion.84
  1358.9 58.9 %reduce-scatter.5.cloned.1.call-done = f32[288,3,320]{2,0,1:T(8,128)} async-done(((f32[1152,3,320]{2,0,1:T(8,128)}), f32[288,3,320]{2,0,1:T(8,128)}) %reduce-scatter.5.cloned.1.call-update) | async-done | bytes 1105936 | tf_op jit(solution)/shard_map/reduce_scatter | solution.py:316
  1417.7 126.2 %reduce-scatter.11.cloned.1.call-done = f32[288,1536]{1,0:T(8,128)} async-done(((f32[1152,1536]{1,0:T(8,128)}), f32[288,1536]{1,0:T(8,128)}) %reduce-scatter.11.cloned.1.call-update) | async-done | bytes 1769488 | tf_op jit(solution)/shard_map/reduce_scatter | solution.py:319
  1543.9 240.2 %reduce-scatter.9.cloned.1.call-done = f32[288,2,1536]{2,0,1:T(8,128)} async-done(((f32[1152,2,1536]{2,0,1:T(8,128)}), f32[288,2,1536]{2,0,1:T(8,128)}) %reduce-scatter.9.cloned.1.call-update) | async-done | bytes 3538960 | tf_op jit(solution)/shard_map/reduce_scatter | solution.py:318
  1784.8 122.5 %all-reduce.20.cloned.1.call-done = f32[1024,1152]{1,0:T(8,128)} async-done(((f32[1024,1152]{1,0:T(8,128)}), f32[1024,1152]{1,0:T(8,128)}) %all-reduce.20.cloned.1.call-update) | async-done | bytes 4718608 | tf_op jit(solution)/shard_map/psum | solution.py:307
  1910.8 18.7 all-reduce.4
  1942.8 107.0 %all-reduce.22.cloned.1.call-done = (f32[288,3,320]{2,0,1:T(8,128)}, f32[288,3,192]{2,0,1:T(8,128)}, f32[288,2,1536]{2,0,1:T(8,128)}, f32[288,1536]{1,0:T(8,128)}) async-done(((f32[288,3,320]{2,0,1:T(8,128)}, f32[288,3,192]{2,0,1:T(8,128)}, f32[288,2,1536]{2,0,1:T(8,128)}, f32[288,1536]{1,0:T(8,128)}), (f32[288,3,320]{2,0,1:T(8,128)}, f32[288,3,192]{2,0,1:T(8,128)}, f32[288,2,1536]{2,0,1:T(8,128)}, ...) | async-done | bytes 7077904 | tf_op jit(solution)/shard_map/psum | solution.py:321
  (435 shorter events, 650.1 us)
Async XLA Ops:
  7.2 60.9 %all-gather.5.cloned.1.call-start = ((), (), s32[]{:S(2)}) async-start(), calls=%async_computation.4 | async-start | bytes 3317760 | tf_op jit(solution)/shard_map/all_gather | solution.py:78
  7.9 257.6 %all-gather.7.cloned.1.call-start = ((), (), s32[]{:S(2)}) async-start(), calls=%async_computation.5 | async-start | bytes 2211840 | tf_op jit(solution)/shard_map/all_gather | solution.py:79
  8.7 26.3 %collective-permute-start.4 = (bf16[1024]{0:T(1024)(128)(2,1)S(1)}, bf16[1024]{0:T(1024)(128)(2,1)S(1)}, u32[]{:S(2)}, u32[]{:S(2)}) collective-permute-start(bf16[1024]{0:T(1024)(128)(2,1)S(1)} %convert_element_type.96), channel_id=1, source_target_pairs={{0,2},{1,3},{4,6},{5,7},{8,10},{9,11},{12,14},{13,15},{16,18},{17,... | collective-permute-start | bytes 6152 | tf_op jit(solution)/shard_map/ppermute | solution.py:20
  14.6 20.3 collective-permute-start.5
  18.2 390.1 %all-reduce.14.cloned.1.call-start = ((), (), s32[]{:S(2)}) async-start(), calls=%async_computation.6 | async-start | bytes 9437184 | tf_op jit(solution)/shard_map/psum | solution.py:175
  21.4 51.5 %copy-start.33 = (f32[1024]{0:T(1024)}, f32[1024]{0:T(1024)S(1)}, u32[]{:S(2)}) copy-start(f32[1024]{0:T(1024)S(1)} %add_rsqrt_fusion.1) | copy-start | bytes 12292
  22.6 61.6 %copy-start.13 = (f32[1024,32]{0,1:T(8,128)}, f32[1024,32]{0,1:T(8,128)S(1)}, u32[]{:S(2)}) copy-start(f32[1024,32]{0,1:T(8,128)S(1)} %get-tuple-element.778) | copy-start | bytes 393220
  73.8 21.4 %collective-permute-start = (bf16[1024,3,64]{0,2,1:T(8,128)(2,1)}, bf16[1024,3,64]{0,2,1:T(8,128)(2,1)S(1)}, u32[]{:S(2)}, u32[]{:S(2)}) collective-permute-start(bf16[1024,3,64]{0,2,1:T(8,128)(2,1)} %pad_maximum_fusion.5), channel_id=1, source_target_pairs={{0,2},{1,3},{4,6},{5,7},{8,10},{9,11},{12,14},{13,15},{16,18},{17,... | collective-permute-start | bytes 1179656 | tf_op jit(solution)/shard_map/ppermute | solution.py:20
  77.0 35.1 %collective-permute-start.1 = (bf16[1024,3,64]{0,2,1:T(8,128)(2,1)}, bf16[1024,3,64]{0,2,1:T(8,128)(2,1)}, u32[]{:S(2)}, u32[]{:S(2)}) collective-permute-start(bf16[1024,3,64]{0,2,1:T(8,128)(2,1)} %pad_maximum_fusion.5), channel_id=1, source_target_pairs={{0,1},{1,2},{2,3},{4,5},{5,6},{6,7},{8,9},{9,10},{10,11},{12,13},{... | collective-permute-start | bytes 1179656 | tf_op jit(solution)/shard_map/ppermute | solution.py:20
  80.1 48.6 %collective-permute-start.2 = (bf16[1024,3,64]{0,2,1:T(8,128)(2,1)S(1)}, bf16[1024,3,64]{0,2,1:T(8,128)(2,1)}, u32[]{:S(2)}, u32[]{:S(2)}) collective-permute-start(bf16[1024,3,64]{0,2,1:T(8,128)(2,1)S(1)} %slice.141), channel_id=1, source_target_pairs={{0,2},{1,3},{4,6},{5,7},{8,10},{9,11},{12,14},{13,15},{16,18},{17,... | collective-permute-start | bytes 1179656 | tf_op jit(solution)/shard_map/ppermute | solution.py:20
  82.2 56.7 %collective-permute-start.3 = (bf16[1024,3,64]{0,2,1:T(8,128)(2,1)S(1)}, bf16[1024,3,64]{0,2,1:T(8,128)(2,1)}, u32[]{:S(2)}, u32[]{:S(2)}) collective-permute-start(bf16[1024,3,64]{0,2,1:T(8,128)(2,1)S(1)} %slice.141), channel_id=1, source_target_pairs={{0,1},{1,2},{2,3},{4,5},{5,6},{6,7},{8,9},{9,10},{10,11},{12,13},{... | collective-permute-start | bytes 1179656 | tf_op jit(solution)/shard_map/ppermute | solution.py:20
  271.6 136.7 %copy-start.4 = (bf16[1024,1152]{1,0:T(8,128)(2,1)S(1)}, bf16[1024,1152]{1,0:T(8,128)(2,1)}, u32[]{:S(2)}) copy-start(bf16[1024,1152]{1,0:T(8,128)(2,1)} %param.18) | copy-start | bytes 7077892
  271.6 266.9 %all-gather.9.cloned.1.call-start = ((), (), s32[]{:S(2)}) async-start(), calls=%async_computation.7 | async-start | bytes 8847360 | tf_op jit(solution)/shard_map/all_gather | solution.py:80
  274.7 333.4 %all-gather.11.cloned.1.call-start = ((), (), s32[]{:S(2)}) async-start(), calls=%async_computation.8 | async-start | bytes 4423680 | tf_op jit(solution)/shard_map/all_gather | solution.py:81
  275.3 475.3 %all-reduce.18.cloned.1.call-start = ((), (), s32[]{:S(2)}) async-start(), calls=%async_computation.10 | async-start | bytes 9437184 | tf_op jit(solution)/shard_map/psum | solution.py:211
  276.0 546.2 %copy-start.37 = (f32[1024]{0:T(1024)}, f32[1024]{0:T(1024)S(1)}, u32[]{:S(2)}) copy-start(f32[1024]{0:T(1024)S(1)} %compare_convert_fusion) | copy-start | bytes 12292
  413.4 408.7 %copy-start.19 = (f32[1024]{0:T(1024)}, f32[1024]{0:T(1024)S(1)}, u32[]{:S(2)}) copy-start(f32[1024]{0:T(1024)S(1)} %add_rsqrt_fusion) | copy-start | bytes 12292
  538.5 69.6 %copy-start.17 = (bf16[1024,1152]{1,0:T(8,128)(2,1)S(1)}, bf16[1024,1152]{1,0:T(8,128)(2,1)}, u32[]{:S(2)}) copy-start(bf16[1024,1152]{1,0:T(8,128)(2,1)} %param.27) | copy-start | bytes 7077892
  632.6 189.6 %all-reduce.16.cloned.1.call-start = ((), (), s32[]{:S(2)}) async-start(), calls=%async_computation.9 | async-start | bytes 4718592 | tf_op jit(solution)/shard_map/psum | solution.py:186
  641.5 717.4 %reduce-scatter.7.cloned.1.call-start = ((), (), s32[]{:S(2)}) async-start(), calls=%async_computation.13 | async-start | bytes 4423680 | tf_op jit(solution)/shard_map/reduce_scatter | solution.py:317
  841.3 576.4 %reduce-scatter.5.cloned.1.call-start = ((), (), s32[]{:S(2)}) async-start(), calls=%async_computation.12 | async-start | bytes 6635520 | tf_op jit(solution)/shard_map/reduce_scatter | solution.py:316
  1263.0 14.7 collective-permute-start.6
  1264.3 38.7 %collective-permute-start.7 = (bf16[1024,3,64]{0,2,1:T(8,128)(2,1)S(1)}, bf16[1024,3,64]{0,2,1:T(8,128)(2,1)S(1)}, u32[]{:S(2)}, u32[]{:S(2)}) collective-permute-start(bf16[1024,3,64]{0,2,1:T(8,128)(2,1)S(1)} %get-tuple-element.771), channel_id=1, source_target_pairs={{2,0},{3,1},{6,4},{7,5},{10,8},{11,9},{14,12},{15,13},{18,16},{19,... | collective-permute-start | bytes 1179656 | tf_op jit(solution)/shard_map/ppermute | solution.py:20
  1265.6 37.7 %collective-permute-start.8 = (bf16[1024,3,64]{0,2,1:T(8,128)(2,1)S(1)}, bf16[1024,3,64]{0,2,1:T(8,128)(2,1)S(1)}, u32[]{:S(2)}, u32[]{:S(2)}) collective-permute-start(bf16[1024,3,64]{0,2,1:T(8,128)(2,1)S(1)} %get-tuple-element.772), channel_id=1, source_target_pairs={{1,0},{2,1},{3,2},{5,4},{6,5},{7,6},{9,8},{10,9},{11,10},{13,12},{... | collective-permute-start | bytes 1179656 | tf_op jit(solution)/shard_map/ppermute | solution.py:20
  1266.9 51.7 %collective-permute-start.9 = (bf16[1024,3,64]{0,2,1:T(8,128)(2,1)S(1)}, bf16[1024,3,64]{0,2,1:T(8,128)(2,1)S(1)}, u32[]{:S(2)}, u32[]{:S(2)}) collective-permute-start(bf16[1024,3,64]{0,2,1:T(8,128)(2,1)S(1)} %get-tuple-element.773), channel_id=1, source_target_pairs={{2,0},{3,1},{6,4},{7,5},{10,8},{11,9},{14,12},{15,13},{18,16},{19,... | collective-permute-start | bytes 1179656 | tf_op jit(solution)/shard_map/ppermute | solution.py:20
  1268.6 50.9 %copy-start.5 = (bf16[1024,1152]{1,0:T(8,128)(2,1)S(1)}, bf16[1024,1152]{1,0:T(8,128)(2,1)}, u32[]{:S(2)}) copy-start(bf16[1024,1152]{1,0:T(8,128)(2,1)} %param.18) | copy-start | bytes 7077892
  1325.5 218.5 %reduce-scatter.11.cloned.1.call-start = ((), (), s32[]{:S(2)}) async-start(), calls=%async_computation.15 | async-start | bytes 8847360 | tf_op jit(solution)/shard_map/reduce_scatter | solution.py:319
  1335.6 448.5 %reduce-scatter.9.cloned.1.call-start = ((), (), s32[]{:S(2)}) async-start(), calls=%async_computation.14 | async-start | bytes 17694720 | tf_op jit(solution)/shard_map/reduce_scatter | solution.py:318
  1350.8 556.5 %all-reduce.20.cloned.1.call-start = ((), (), s32[]{:S(2)}) async-start(), calls=%async_computation.11 | async-start | bytes 9437184 | tf_op jit(solution)/shard_map/psum | solution.py:307
  1358.8 691.1 %all-reduce.22.cloned.1.call-start = ((), (), s32[]{:S(2)}) async-start(), calls=%async_computation.16 | async-start | bytes 15040512 | tf_op jit(solution)/shard_map/psum | solution.py:321
  1784.1 123.2 %copy-start.32 = (f32[1152]{0:T(1024)S(1)}, f32[1152]{0:T(1024)}, u32[]{:S(2)}) copy-start(f32[1152]{0:T(1024)} %copy-done.30) | copy-start | bytes 13828
  1784.8 126.1 %copy-start.36 = (f32[1152]{0:T(1024)S(1)}, f32[1152]{0:T(1024)}, u32[]{:S(2)}) copy-start(f32[1152]{0:T(1024)} %get-tuple-element.623) | copy-start | bytes 13828
  (67 other events, 570.3 us)
Sparse Core Ops, SparseCore 0:
  9.6 58.4 all-gather.4
  69.7 63.5 all-gather.6
  271.7 136.5 all-reduce.13
  410.3 128.1 all-gather.8
  539.9 68.1 all-gather.10
  632.7 117.8 all-reduce.17
  753.4 68.6 all-reduce.15
  841.5 66.4 reduce-scatter.6
  1325.6 92.0 reduce-scatter.4
  1419.9 124.0 reduce-scatter.10
  1546.3 237.7 reduce-scatter.8
  1787.0 120.2 all-reduce.19
  1909.9 139.9 all-reduce.21
where the time goes:
time: 2080 us; the launch traced here: 2070 us
  waiting for transfers between devices  1270 us (61%)
  matrix products  396 us (19%)
  other arithmetic  226 us (11%)
  local copies, waits for them, and re-layouts  95 us (5%)
  blocking collectives  36 us (2%)
  starting transfers between devices  25.4 us (1%)
    reduce_scatter x1, waiting for transfers between devices, local(): lax.psum_scatter(gate_up_grad, 'col', scatter_dimension=0, tiled=True)  240 us
    psum x1, waiting for transfers between devices, local(): lax.psum(jnp.einsum('the,dhe->td', context_low, full_out, preferred_eleme...  132 us
    reduce_scatter x1, waiting for transfers between devices, local(): lax.psum_scatter(down_grad, 'col', scatter_dimension=0, tiled=True)  126 us
    all_gather x1, waiting for transfers between devices, local(): lax.all_gather(w_gate_up, 'col', axis=0, tiled=True)  125 us
    psum x1, waiting for transfers between devices, local(): lax.psum(jnp.einsum('the,dhe->td', grad_projected, back_qkv, preferred_el...  122 us
    convert_element_type x6, other arithmetic, backward_block(): grad_scores = (probs * (grad_probs - inner_sum)).astype(jnp.bfloat16)  107 us
    psum x1, waiting for transfers between devices, local(): lax.psum((share_one, share_two, share_qkv, share_out, share_gate_up, shar...  107 us
    psum x1, waiting for transfers between devices, local(): lax.psum(jnp.einsum('tcf,dcf->td', grad_gate_up, back_gate_up, preferred_...  105 us
  transfers between devices with their start and end apart: 23, of which 18 were waited for; matrix products, arithmetic and copies ran while one was open for 31% of the time, Pallas kernels for 0%

commit v1 on v0

--- a/solution.py
+++ b/solution.py
@@ -12,6 +12,12 @@
 epsilon = 1e-05
 rope_base = 10000.0
 masked_score = -1e30
+
+
+def open_kinds(u, out_dim):
+    x_now = list(u.shape[1:])
+    x_now[out_dim] *= u.shape[0]
+    return jnp.moveaxis(u, 0, out_dim).reshape(x_now)
 
 
 def shifted(value, axis, steps):
@@ -72,13 +78,33 @@
     group_width = QUERY_HEADS // KEY_VALUE_HEADS
     query_feature_width = group_width * HEAD_WIDTH
     score_scale = 1.0 / math.sqrt(HEAD_WIDTH)
+
+    def paths_update(along_dim, bus_axis, local_x):
+        axis_total = lax.axis_size(bus_axis)
+        frames = tuple(((s, (s + 1) % axis_total) for s in range(axis_total)))
+        arrivals = tuple(((k0, b) for b, k0 in frames))
+        aux, mat_out = ([], [])
+        for to_i in range(axis_total - 1):
+            if to_i % 2 == 0:
+                near = lax.ppermute(aux[-1] if aux else local_x, axis_name=bus_axis, perm=frames)
+                aux.append(near)
+            else:
+                item_now = lax.ppermute(
+                    mat_out[-1] if mat_out else local_x, axis_name=bus_axis, perm=arrivals
+                )
+                mat_out.append(item_now)
+        formed = jnp.stack([*aux[::-1], local_x, *mat_out], axis=0)
+        front = lax.axis_index(bus_axis) - len(aux)
+        formed = formed[(jnp.arange(axis_total) - front) % axis_total]
+        return open_kinds(formed, along_dim)
+
     gain_one, gain_two, full_qkv, full_out, full_gate_up, full_down = (
         lax.all_gather(norm1_gain, "col", axis=0, tiled=True),
         lax.all_gather(norm2_gain, "col", axis=0, tiled=True),
         lax.all_gather(query_key_value_weight, "col", axis=0, tiled=True),
         lax.all_gather(output_weight, "col", axis=0, tiled=True),
         lax.all_gather(w_gate_up, "col", axis=0, tiled=True),
-        lax.all_gather(w_down, "col", axis=0, tiled=True),
+        paths_update(0, "col", w_down),
     )
     gain_one = gain_one.astype(jnp.float32)
     gain_two = gain_two.astype(jnp.float32)

time: 2080 us -> 1970 us (0.947)
  matrix products: 396 us -> 316 us
  other arithmetic: 226 us -> 197 us
    psum x1, waiting for transfers between devices: 105 us -> 33.6 us  [local(): lax.psum(jnp.einsum('tcf,dcf->td', grad_gate_up, back_gate_up, preferred_...]
    ppermute x0 -> x3, waiting for transfers between devices: none -> 56.5 us  [the longest x2 41.3 us: paths_update(): lax.ppermute(aux[-1] if aux else local_x, axis_name=bus_axis, perm=frames)]
    dot_general x6, matrix products: 57.8 us -> 25.4 us  [backward_block(): jnp.einsum('gqk,qgd->kd', probs.astype(jnp.bfloat16), grad_block, preferr...]
    dot_general x12, matrix products: 69.6 us -> 37.5 us  [scores_for(): jnp.einsum('qgd,kd->gqk', query_block, head_keys, preferred_element_type=...]
    while x78 -> x36, local copies, waits for them, and re-layouts: 10.4 us -> 38.9 us
    convert_element_type x6, other arithmetic: 107 us -> 83.6 us  [backward_block(): grad_scores = (probs * (grad_probs - inner_sum)).astype(jnp.bfloat16)]
    dot_general x6, matrix products: 33.9 us -> 11.2 us  [backward_block(): jnp.einsum('gqk,qgd->kd', grad_scores, query_block, preferred_element_typ...]
  transfers between devices with their start and end apart: 23 -> 26, of which waited for: 18 -> 20; matrix products, arithmetic and copies ran while one was open for 31% -> 27% of each run, Pallas kernels for 0% -> 0%
where the time goes in v1:
time: 1970 us; the launch traced here: 1960 us
  waiting for transfers between devices  1250 us (63%)
  matrix products  316 us (16%)
  other arithmetic  197 us (10%)
  local copies, waits for them, and re-layouts  115 us (6%)
  blocking collectives  35.9 us (2%)
  starting transfers between devices  28.7 us (1%)
    reduce_scatter x1, waiting for transfers between devices, local(): lax.psum_scatter(gate_up_grad, 'col', scatter_dimension=0, tiled=True)  240 us
    psum x1, waiting for transfers between devices, local(): lax.psum(jnp.einsum('the,dhe->td', context_low, full_out, preferred_eleme...  135 us
    reduce_scatter x1, waiting for transfers between devices, local(): lax.psum_scatter(down_grad, 'col', scatter_dimension=0, tiled=True)  126 us
    all_gather x1, waiting for transfers between devices, local(): lax.all_gather(w_gate_up, 'col', axis=0, tiled=True)  125 us
    psum x1, waiting for transfers between devices, local(): lax.psum(jnp.einsum('the,dhe->td', grad_projected, back_qkv, preferred_el...  123 us
    psum x1, waiting for transfers between devices, local(): lax.psum((share_one, share_two, share_qkv, share_out, share_gate_up, shar...  107 us
    ppermute x10, waiting for transfers between devices, shifted(): lax.ppermute(value, axis, [(source, source + steps) for source in range(l...  96.8 us
    convert_element_type x6, other arithmetic, backward_block(): grad_scores = (probs * (grad_probs - inner_sum)).astype(jnp.bfloat16)  83.6 us
  transfers between devices with their start and end apart: 26, of which 20 were waited for; matrix products, arithmetic and copies ran while one was open for 27% of the time, Pallas kernels for 0%

profile of v1, /device:TPU:0, one launch (start us, length us, event | category | flops | bytes accessed | tf_op | source)
XLA Modules:
  0.0 1963.4 jit_solution(5131999138605579838)
XLA Ops:
  34.4 33.7 %all-gather.5.cloned.1.call-done = bf16[1152,3,320]{2,0,1:T(8,128)(2,1)} async-done(((bf16[288,3,320]{2,0,1:T(8,128)(2,1)}), bf16[1152,3,320]{2,0,1:T(8,128)(2,1)}) %all-gather.5.cloned.1.call-update) | async-done | bytes 2211856 | tf_op jit(solution)/shard_map/all_gather | solution.py:104
  93.8 16.9 collective-permute-done
  112.7 14.6 collective-permute-done.3
  139.9 116.6 %while.68 = (s32[]{:T(128)}, bf16[3,2,512,3,64]{2,4,3,1,0:T(8,128)(2,1)}, f32[3,2,3,512]{3,2,1,0:T(4,128)}, bf16[3,2,512,3,64]{2,4,3,1,0:T(8,128)(2,1)}, bf16[3,...) while((s32[]{:T(128)}, ...), condition=%wide.region_7.8_spmd.clone.clone.clone, body=%wide.region_2.7_spmd.clone.clone.sunk.clone | while | flops 1275651072 | bytes 67577272 | solution.py:195
  142.4 35.2 %while.67 = (s32[]{:T(128)}, bf16[2,512,3,64]{1,3,2,0:T(8,128)(2,1)S(1)}, f32[2,3,512]{2,1,0:T(4,128)S(1)}, s32[3072]{0:T(1024)S(1)}, s32[2,512]{1,0:T(2,128)S(1...) while((s32[]{:T(128)}, ...), condition=%wide.region_6.6_spmd, body=%wide.region_3.5_spmd.sunk | while | flops 1275592704 | bytes 64383128 | solution.py:193
  181.2 35.2 %while.67 = (s32[]{:T(128)}, bf16[2,512,3,64]{1,3,2,0:T(8,128)(2,1)S(1)}, f32[2,3,512]{2,1,0:T(4,128)S(1)}, s32[3072]{0:T(1024)S(1)}, s32[2,512]{1,0:T(2,128)S(1...) while((s32[]{:T(128)}, ...), condition=%wide.region_6.6_spmd, body=%wide.region_3.5_spmd.sunk | while | flops 1275592704 | bytes 64383128 | solution.py:193
  220.0 35.2 %while.67 = (s32[]{:T(128)}, bf16[2,512,3,64]{1,3,2,0:T(8,128)(2,1)S(1)}, f32[2,3,512]{2,1,0:T(4,128)S(1)}, s32[3072]{0:T(1024)S(1)}, s32[2,512]{1,0:T(2,128)S(1...) while((s32[]{:T(128)}, ...), condition=%wide.region_6.6_spmd, body=%wide.region_3.5_spmd.sunk | while | flops 1275592704 | bytes 64383128 | solution.py:193
  270.4 135.1 %all-reduce.14.cloned.1.call-done = f32[1024,1152]{1,0:T(8,128)} async-done(((f32[1024,1152]{1,0:T(8,128)}), f32[1024,1152]{1,0:T(8,128)}) %all-reduce.14.cloned.1.call-update) | async-done | bytes 4718608 | tf_op jit(solution)/shard_map/psum | solution.py:201
  410.6 125.1 %all-gather.9.cloned.1.call-done = bf16[1152,2,1536]{2,0,1:T(8,128)(2,1)} async-done(((bf16[288,2,1536]{2,0,1:T(8,128)(2,1)}), bf16[1152,2,1536]{2,0,1:T(8,128)(2,1)}) %all-gather.9.cloned.1.call-update) | async-done | bytes 7077904 | tf_op jit(solution)/shard_map/all_gather | solution.py:106
  535.7 15.2 fusion.115
  550.9 54.4 %all-gather.11.cloned.1.call-done = bf16[1152,1536]{1,0:T(8,128)(2,1)} async-done(((bf16[288,1536]{1,0:T(8,128)(2,1)}), bf16[1152,1536]{1,0:T(8,128)(2,1)}) %all-gather.11.cloned.1.call-update) | async-done | bytes 3538960 | tf_op jit(solution)/shard_map/all_gather | solution.py:223
  633.1 20.5 %collective-permute-done.6 = bf16[288,1536]{1,0:T(8,128)(2,1)S(1)} collective-permute-done((bf16[288,1536]{1,0:T(8,128)(2,1)S(1)}, bf16[288,1536]{1,0:T(8,128)(2,1)S(1)}, u32[]{:S(2)}, u32[]{:S(2)}) %collective-permute-start.6) | collective-permute-done | bytes 884768 | tf_op jit(solution)/shard_map/ppermute | solution.py:89
  654.3 15.2 collective-permute-done.8
  669.4 20.8 %collective-permute-done.7 = bf16[288,1536]{1,0:T(8,128)(2,1)S(1)} collective-permute-done((bf16[288,1536]{1,0:T(8,128)(2,1)S(1)}, bf16[288,1536]{1,0:T(8,128)(2,1)S(1)}, u32[]{:S(2)}, u32[]{:S(2)}) %collective-permute-start.7) | collective-permute-done | bytes 884768 | tf_op jit(solution)/shard_map/ppermute | solution.py:89
  712.5 33.6 %all-reduce.18.cloned.1.call-done = f32[1024,1152]{1,0:T(8,128)} async-done(((f32[1024,1152]{1,0:T(8,128)}), f32[1024,1152]{1,0:T(8,128)}) %all-reduce.18.cloned.1.call-update) | async-done | bytes 4718608 | tf_op jit(solution)/shard_map/psum | solution.py:237
  752.2 65.5 %all-reduce.16.cloned.1.call-done = bf16[1024,1152]{1,0:T(8,128)(2,1)} async-done(((bf16[1024,1152]{1,0:T(8,128)(2,1)}), bf16[1024,1152]{1,0:T(8,128)(2,1)}) %all-reduce.16.cloned.1.call-update) | async-done | bytes 2359312 | tf_op jit(solution)/shard_map/psum | solution.py:212
  837.0 319.0 %while.70 = (s32[]{:T(128)}, f32[3,2,512,3,64]{2,4,3,1,0:T(8,128)}, f32[3,3072,64]{1,2,0:T(8,128)}, f32[3,3072,64]{1,2,0:T(8,128)}, bf16[3,2,512,3,64]{2,4,3,1,0...) while((s32[]{:T(128)}, f32[3,2,512,3,64]{2,4,3,1,0:T(8,128)}, ...), condition=%wide.region_17.18_spmd.clone.clone.clone, body=%wide.region_13.17_spmd.clone.clone.sunk.clone | while | flops 3102827520 | bytes 243132016 | solution.py:298
  842.1 98.1 %while.69 = (s32[]{:T(128)}, f32[3072,64]{0,1:T(8,128)S(1)}, f32[3072,64]{0,1:T(8,128)}, f32[2,512,3,64]{1,3,2,0:T(8,128)S(1)}, s32[3072]{0:T(1024)S(1)}, /*inde...) while((s32[]{:T(128)}, f32[3072,64]{0,1:T(8,128)S(1)}, ...), condition=%wide.region_16.16_spmd.clone, body=%wide.region_14.15_spmd.clone.sunk | while | flops 3102769152 | bytes 235223312 | solution.py:291
  872.4 14.0 fusion.180
  921.4 13.9 fusion.180
  948.4 97.9 %while.69 = (s32[]{:T(128)}, f32[3072,64]{0,1:T(8,128)S(1)}, f32[3072,64]{0,1:T(8,128)}, f32[2,512,3,64]{1,3,2,0:T(8,128)S(1)}, s32[3072]{0:T(1024)S(1)}, /*inde...) while((s32[]{:T(128)}, f32[3072,64]{0,1:T(8,128)S(1)}, ...), condition=%wide.region_16.16_spmd.clone, body=%wide.region_14.15_spmd.clone.sunk | while | flops 3102769152 | bytes 235223312 | solution.py:291
  978.6 13.9 fusion.180
  1054.6 97.9 %while.69 = (s32[]{:T(128)}, f32[3072,64]{0,1:T(8,128)S(1)}, f32[3072,64]{0,1:T(8,128)}, f32[2,512,3,64]{1,3,2,0:T(8,128)S(1)}, s32[3072]{0:T(1024)S(1)}, /*inde...) while((s32[]{:T(128)}, f32[3072,64]{0,1:T(8,128)S(1)}, ...), condition=%wide.region_16.16_spmd.clone, body=%wide.region_14.15_spmd.clone.sunk | while | flops 3102769152 | bytes 235223312 | solution.py:291
  1165.3 16.5 collective-permute-done.9
  1181.8 33.4 %collective-permute-done.10 = bf16[1024,3,64]{0,2,1:T(8,128)(2,1)S(1)} collective-permute-done((bf16[1024,3,64]{0,2,1:T(8,128)(2,1)S(1)}, bf16[1024,3,64]{0,2,1:T(8,128)(2,1)S(1)}, u32[]{:S(2)}, u32[]{:S(2)}) %collective-permute-start.10) | collective-permute-done | bytes 393248 | tf_op jit(solution)/shard_map/ppermute | solution.py:26
  1236.9 14.7 fusion.91
  1259.7 54.9 %reduce-scatter.5.cloned.1.call-done = f32[288,3,320]{2,0,1:T(8,128)} async-done(((f32[1152,3,320]{2,0,1:T(8,128)}), f32[288,3,320]{2,0,1:T(8,128)}) %reduce-scatter.5.cloned.1.call-update) | async-done | bytes 1105936 | tf_op jit(solution)/shard_map/reduce_scatter | solution.py:342
  1314.7 126.2 %reduce-scatter.11.cloned.1.call-done = f32[288,1536]{1,0:T(8,128)} async-done(((f32[1152,1536]{1,0:T(8,128)}), f32[288,1536]{1,0:T(8,128)}) %reduce-scatter.11.cloned.1.call-update) | async-done | bytes 1769488 | tf_op jit(solution)/shard_map/reduce_scatter | solution.py:345
  1440.9 240.2 %reduce-scatter.9.cloned.1.call-done = f32[288,2,1536]{2,0,1:T(8,128)} async-done(((f32[1152,2,1536]{2,0,1:T(8,128)}), f32[288,2,1536]{2,0,1:T(8,128)}) %reduce-scatter.9.cloned.1.call-update) | async-done | bytes 3538960 | tf_op jit(solution)/shard_map/reduce_scatter | solution.py:344
  1681.7 122.5 %all-reduce.20.cloned.1.call-done = f32[1024,1152]{1,0:T(8,128)} async-done(((f32[1024,1152]{1,0:T(8,128)}), f32[1024,1152]{1,0:T(8,128)}) %all-reduce.20.cloned.1.call-update) | async-done | bytes 4718608 | tf_op jit(solution)/shard_map/psum | solution.py:333
  1807.8 18.7 all-reduce.4
  1839.7 107.1 %all-reduce.22.cloned.1.call-done = (f32[288,3,320]{2,0,1:T(8,128)}, f32[288,3,192]{2,0,1:T(8,128)}, f32[288,2,1536]{2,0,1:T(8,128)}, f32[288,1536]{1,0:T(8,128)}) async-done(((f32[288,3,320]{2,0,1:T(8,128)}, f32[288,3,192]{2,0,1:T(8,128)}, f32[288,2,1536]{2,0,1:T(8,128)}, f32[288,1536]{1,0:T(8,128)}), (f32[288,3,320]{2,0,1:T(8,128)}, f32[288,3,192]{2,0,1:T(8,128)}, f32[288,2,1536]{2,0,1:T(8,128)}, ...) | async-done | bytes 7077904 | tf_op jit(solution)/shard_map/psum | solution.py:347
  (421 shorter events, 619.1 us)
Async XLA Ops:
  7.2 60.9 %all-gather.5.cloned.1.call-start = ((), (), s32[]{:S(2)}) async-start(), calls=%async_computation.4 | async-start | bytes 3317760 | tf_op jit(solution)/shard_map/all_gather | solution.py:104
  7.9 252.2 %all-gather.7.cloned.1.call-start = ((), (), s32[]{:S(2)}) async-start(), calls=%async_computation.5 | async-start | bytes 2211840 | tf_op jit(solution)/shard_map/all_gather | solution.py:105
  8.7 25.7 %collective-permute-start.5 = (bf16[1024]{0:T(1024)(128)(2,1)S(1)}, bf16[1024]{0:T(1024)(128)(2,1)S(1)}, u32[]{:S(2)}, u32[]{:S(2)}) collective-permute-start(bf16[1024]{0:T(1024)(128)(2,1)S(1)} %convert_element_type.101), channel_id=1, source_target_pairs={{0,1},{1,2},{2,3},{4,5},{5,6},{6,7},{8,9},{9,10},{10,11},{12,13},{... | collective-permute-start | bytes 6152 | tf_op jit(solution)/shard_map/ppermute | solution.py:26
  13.6 20.8 %collective-permute-start.4 = (bf16[1024]{0:T(1024)(128)(2,1)S(1)}, bf16[1024]{0:T(1024)(128)(2,1)S(1)}, u32[]{:S(2)}, u32[]{:S(2)}) collective-permute-start(bf16[1024]{0:T(1024)(128)(2,1)S(1)} %convert_element_type.101), channel_id=1, source_target_pairs={{0,2},{1,3},{4,6},{5,7},{8,10},{9,11},{12,14},{13,15},{16,18},{17,... | collective-permute-start | bytes 6152 | tf_op jit(solution)/shard_map/ppermute | solution.py:26
  18.2 387.3 %all-reduce.14.cloned.1.call-start = ((), (), s32[]{:S(2)}) async-start(), calls=%async_computation.6 | async-start | bytes 9437184 | tf_op jit(solution)/shard_map/psum | solution.py:201
  74.1 19.6 collective-permute-start.1
  75.9 34.7 %collective-permute-start = (bf16[1024,3,64]{0,2,1:T(8,128)(2,1)}, bf16[1024,3,64]{0,2,1:T(8,128)(2,1)}, u32[]{:S(2)}, u32[]{:S(2)}) collective-permute-start(bf16[1024,3,64]{0,2,1:T(8,128)(2,1)} %pad_maximum_fusion.6), channel_id=1, source_target_pairs={{0,2},{1,3},{4,6},{5,7},{8,10},{9,11},{12,14},{13,15},{16,18},{17,... | collective-permute-start | bytes 1179656 | tf_op jit(solution)/shard_map/ppermute | solution.py:26
  80.1 47.3 %collective-permute-start.3 = (bf16[1024,3,64]{0,2,1:T(8,128)(2,1)S(1)}, bf16[1024,3,64]{0,2,1:T(8,128)(2,1)S(1)}, u32[]{:S(2)}, u32[]{:S(2)}) collective-permute-start(bf16[1024,3,64]{0,2,1:T(8,128)(2,1)S(1)} %slice.147), channel_id=1, source_target_pairs={{0,1},{1,2},{2,3},{4,5},{5,6},{6,7},{8,9},{9,10},{10,11},{12,13},{... | collective-permute-start | bytes 1179656 | tf_op jit(solution)/shard_map/ppermute | solution.py:26
  81.8 56.0 %collective-permute-start.2 = (bf16[1024,3,64]{0,2,1:T(8,128)(2,1)S(1)}, bf16[1024,3,64]{0,2,1:T(8,128)(2,1)}, u32[]{:S(2)}, u32[]{:S(2)}) collective-permute-start(bf16[1024,3,64]{0,2,1:T(8,128)(2,1)S(1)} %slice.147), channel_id=1, source_target_pairs={{0,2},{1,3},{4,6},{5,7},{8,10},{9,11},{12,14},{13,15},{16,18},{17,... | collective-permute-start | bytes 1179656 | tf_op jit(solution)/shard_map/ppermute | solution.py:26
  266.6 138.9 %copy-start.2 = (bf16[1024,1152]{1,0:T(8,128)(2,1)S(1)}, bf16[1024,1152]{1,0:T(8,128)(2,1)}, u32[]{:S(2)}) copy-start(bf16[1024,1152]{1,0:T(8,128)(2,1)} %param.18) | copy-start | bytes 7077892
  266.6 269.1 %all-gather.9.cloned.1.call-start = ((), (), s32[]{:S(2)}) async-start(), calls=%async_computation.7 | async-start | bytes 8847360 | tf_op jit(solution)/shard_map/all_gather | solution.py:106
  269.7 335.6 %all-gather.11.cloned.1.call-start = ((), (), s32[]{:S(2)}) async-start(), calls=%async_computation.9 | async-start | bytes 4423680 | tf_op jit(solution)/shard_map/all_gather | solution.py:223
  270.3 475.8 %all-reduce.18.cloned.1.call-start = ((), (), s32[]{:S(2)}) async-start(), calls=%async_computation.10 | async-start | bytes 9437184 | tf_op jit(solution)/shard_map/psum | solution.py:237
  270.4 265.3 %copy-start.25 = (f32[1152]{0:T(1024)}, f32[1152]{0:T(1024)S(1)}, u32[]{:S(2)}) copy-start(f32[1152]{0:T(1024)S(1)} %convert_element_type.105) | copy-start | bytes 13828
  270.4 334.9 %copy-start.42 = (f32[1024]{0:T(1024)}, f32[1024]{0:T(1024)S(1)}, u32[]{:S(2)}) copy-start(f32[1024]{0:T(1024)S(1)} %compare_convert_fusion) | copy-start | bytes 12292
  410.6 407.1 %copy-start.18 = (f32[1024]{0:T(1024)}, f32[1024]{0:T(1024)S(1)}, u32[]{:S(2)}) copy-start(f32[1024]{0:T(1024)S(1)} %add_rsqrt_fusion) | copy-start | bytes 12292
  628.1 189.6 %all-reduce.16.cloned.1.call-start = ((), (), s32[]{:S(2)}) async-start(), calls=%async_computation.8 | async-start | bytes 4718592 | tf_op jit(solution)/shard_map/psum | solution.py:212
  629.2 24.3 %collective-permute-start.6 = (bf16[288,1536]{1,0:T(8,128)(2,1)S(1)}, bf16[288,1536]{1,0:T(8,128)(2,1)S(1)}, u32[]{:S(2)}, u32[]{:S(2)}) collective-permute-start(bf16[288,1536]{1,0:T(8,128)(2,1)S(1)} %copy-done.9), channel_id=1, source_target_pairs={{0,1},{1,2},{2,3},{3,0},{4,5},{5,6},{6,7},{7,4},{8,9},{9,10},{10,1... | collective-permute-start | bytes 2654216 | tf_op jit(solution)/shard_map/ppermute | solution.py:89
  629.2 40.2 %collective-permute-start.8 = (bf16[288,1536]{1,0:T(8,128)(2,1)S(1)}, bf16[288,1536]{1,0:T(8,128)(2,1)S(1)}, u32[]{:S(2)}, u32[]{:S(2)}) collective-permute-start(bf16[288,1536]{1,0:T(8,128)(2,1)S(1)} %copy-done.9), channel_id=1, source_target_pairs={{1,0},{2,1},{3,2},{0,3},{5,4},{6,5},{7,6},{4,7},{9,8},{10,9},{11,1... | collective-permute-start | bytes 2654216 | tf_op jit(solution)/shard_map/ppermute | solution.py:92
  653.6 36.7 %collective-permute-start.7 = (bf16[288,1536]{1,0:T(8,128)(2,1)S(1)}, bf16[288,1536]{1,0:T(8,128)(2,1)S(1)}, u32[]{:S(2)}, u32[]{:S(2)}) collective-permute-start(bf16[288,1536]{1,0:T(8,128)(2,1)S(1)} %collective-permute-done.6), channel_id=1, source_target_pairs={{0,1},{1,2},{2,3},{3,0},{4,5},{5,6},{6,7},{7,4},{8,9},{9,10},{10,1... | collective-permute-start | bytes 2654216 | tf_op jit(solution)/shard_map/ppermute | solution.py:89
  708.9 550.8 %reduce-scatter.7.cloned.1.call-start = ((), (), s32[]{:S(2)}) async-start(), calls=%async_computation.13 | async-start | bytes 4423680 | tf_op jit(solution)/shard_map/reduce_scatter | solution.py:343
  836.9 477.7 %reduce-scatter.5.cloned.1.call-start = ((), (), s32[]{:S(2)}) async-start(), calls=%async_computation.12 | async-start | bytes 6635520 | tf_op jit(solution)/shard_map/reduce_scatter | solution.py:342
  1159.5 56.0 %collective-permute-start.11 = (bf16[1024,3,64]{0,2,1:T(8,128)(2,1)S(1)}, bf16[1024,3,64]{0,2,1:T(8,128)(2,1)S(1)}, u32[]{:S(2)}, u32[]{:S(2)}) collective-permute-start(bf16[1024,3,64]{0,2,1:T(8,128)(2,1)S(1)} %get-tuple-element.771), channel_id=1, source_target_pairs={{1,0},{2,1},{3,2},{5,4},{6,5},{7,6},{9,8},{10,9},{11,10},{13,12},{... | collective-permute-start | bytes 1179656 | tf_op jit(solution)/shard_map/ppermute | solution.py:26
  1160.8 54.7 %collective-permute-start.12 = (bf16[1024,3,64]{0,2,1:T(8,128)(2,1)S(1)}, bf16[1024,3,64]{0,2,1:T(8,128)(2,1)S(1)}, u32[]{:S(2)}, u32[]{:S(2)}) collective-permute-start(bf16[1024,3,64]{0,2,1:T(8,128)(2,1)S(1)} %get-tuple-element.772), channel_id=1, source_target_pairs={{2,0},{3,1},{6,4},{7,5},{10,8},{11,9},{14,12},{15,13},{18,16},{19,... | collective-permute-start | bytes 1179656 | tf_op jit(solution)/shard_map/ppermute | solution.py:26
  1162.2 19.6 collective-permute-start.9
  1163.5 51.7 %collective-permute-start.10 = (bf16[1024,3,64]{0,2,1:T(8,128)(2,1)S(1)}, bf16[1024,3,64]{0,2,1:T(8,128)(2,1)S(1)}, u32[]{:S(2)}, u32[]{:S(2)}) collective-permute-start(bf16[1024,3,64]{0,2,1:T(8,128)(2,1)S(1)} %get-tuple-element.770), channel_id=1, source_target_pairs={{2,0},{3,1},{6,4},{7,5},{10,8},{11,9},{14,12},{15,13},{18,16},{19,... | collective-permute-start | bytes 1179656 | tf_op jit(solution)/shard_map/ppermute | solution.py:26
  1222.4 218.5 %reduce-scatter.11.cloned.1.call-start = ((), (), s32[]{:S(2)}) async-start(), calls=%async_computation.15 | async-start | bytes 8847360 | tf_op jit(solution)/shard_map/reduce_scatter | solution.py:345
  1236.3 444.8 %reduce-scatter.9.cloned.1.call-start = ((), (), s32[]{:S(2)}) async-start(), calls=%async_computation.14 | async-start | bytes 17694720 | tf_op jit(solution)/shard_map/reduce_scatter | solution.py:344
  1251.7 552.5 %all-reduce.20.cloned.1.call-start = ((), (), s32[]{:S(2)}) async-start(), calls=%async_computation.11 | async-start | bytes 9437184 | tf_op jit(solution)/shard_map/psum | solution.py:333
  1259.7 687.1 %all-reduce.22.cloned.1.call-start = ((), (), s32[]{:S(2)}) async-start(), calls=%async_computation.16 | async-start | bytes 15040512 | tf_op jit(solution)/shard_map/psum | solution.py:347
  1681.0 123.2 %copy-start.37 = (f32[1152]{0:T(1024)S(1)}, f32[1152]{0:T(1024)}, u32[]{:S(2)}) copy-start(f32[1152]{0:T(1024)} %copy-done.35) | copy-start | bytes 13828
  1681.7 126.1 %copy-start.41 = (f32[1152]{0:T(1024)S(1)}, f32[1152]{0:T(1024)}, u32[]{:S(2)}) copy-start(f32[1152]{0:T(1024)} %get-tuple-element.623) | copy-start | bytes 13828
  (58 other events, 1004.9 us)
Sparse Core Ops, SparseCore 0:
  9.6 58.4 all-gather.4
  69.7 63.9 all-gather.6
  266.7 138.7 all-reduce.13
  407.5 128.1 all-gather.8
  537.1 68.1 all-gather.10
  628.2 117.8 all-reduce.17
  749.0 68.6 all-reduce.15
  837.1 66.4 reduce-scatter.6
  1222.5 92.0 reduce-scatter.4
  1316.8 124.0 reduce-scatter.10
  1443.2 237.7 reduce-scatter.8
  1683.9 120.2 all-reduce.19
  1806.9 139.9 all-reduce.21
